TPU v7x, 512 devices: a whole 4x8x8 slice. The times are simulated.
512 devices in a mesh: dp: 4 (over y_lo), head: 8 (over z), ctx: 16 (over x, y_hi, core).
Axes of the slice: x: 4, y: 8 (y_hi: 2, y_lo: 4; y = y_hi * 4 + y_lo), z: 8, core: 2. Of those that a mesh axis runs over, the one named last changes fastest.
Arguments:
- query_rows: bfloat16 [16384, 8192], P(('dp', 'ctx'), 'head'), parts along dimension 0, may hold values from -12 to 12
- key_rows: bfloat16 [16384, 1024], P(('dp', 'ctx'), 'head'), parts along dimension 0, may hold values from -4 to 4
- stored_value_rows: bfloat16 [16384, 1024], P(('dp', 'ctx'), 'head'), parts along dimension 0, may hold values from -6 to 6
- out_grad: bfloat16 [16384, 8192], P(('dp', 'ctx'), 'head'), parts along dimension 0, may hold values from -6 to 6
- block_table: int32 [64, 2], P('dp'), parts along dimension 0, may hold values from 0 to 31, as said below
- pattern: int32 [128, 10], P('dp'), parts along dimension 0, may hold values from 0 to 31, as said below
Outputs:
- attended: bfloat16 [16384, 8192], P(('dp', 'ctx'), 'head'), parts along dimension 0
- query_grad: bfloat16 [16384, 8192], P(('dp', 'ctx'), 'head'), parts along dimension 0
- key_grad: bfloat16 [16384, 1024], P(('dp', 'ctx'), 'head'), parts along dimension 0
- value_grad: bfloat16 [16384, 1024], P(('dp', 'ctx'), 'head'), parts along dimension 0
There are 4 independent parts, one for each index of `dp`. A program takes and returns all parts, laid end to end along the dimension named above; each array names one. Nothing has to cross between parts.
Inputs may be any that keep to these rules, and one draw needn't show every extreme that they name: `pattern`: row b lists the key blocks that sequence block b reads, in no order; every entry is at most b; b, max(b - 1, 0) and 0 are always listed; repeated entries count once. `block_table`: each sequence block is held by exactly one storage block, and sequence blocks b and 31 - b are held by the same ctx index.
All inputs are finite; a program needn't handle non-finite values.
Results may differ from a plain program's by a relative error of at most 0.015.
Values may be sent and summed in bfloat16 or wider, within the bound.
No kernel may reach another device: no remote copies, remote signals or barrier semaphores. Data moves between devices by JAX's collectives and lax.ppermute only.
A program may use at most 64 MiB of HBM per device.

v0:
```python
import jax
import jax.numpy as jnp
from jax import lax
from jax.sharding import PartitionSpec as P

HEAD_SIZE = 128
BLK = 128


def slot_layout(block_table, pattern, held_seq):
    blocks = pattern.shape[0]
    slots = pattern.shape[1]
    block_ids = jnp.arange(blocks, dtype=jnp.int32)
    store_seq = block_table.reshape(-1)
    inverse = jnp.sum(
        jnp.where(store_seq[:, None] == block_ids[None, :], block_ids[:, None], 0), axis=0
    )
    onehot = (held_seq[:, None] == block_ids[None, :]).astype(jnp.int32)
    held_pattern = jnp.sum(onehot[:, :, None] * pattern[None, :, :], axis=1)
    key_store = jnp.sum(
        jnp.where(held_pattern[:, :, None] == block_ids[None, None, :], inverse[None, None, :], 0),
        axis=2,
    )
    same = held_pattern[:, :, None] == held_pattern[:, None, :]
    slot_ids = jnp.arange(slots, dtype=jnp.int32)
    before = slot_ids[None, :] < slot_ids[:, None]
    live_slot = jnp.logical_not(jnp.any(same & before[None], axis=2))
    inner = jnp.arange(BLK, dtype=jnp.int32)
    query_pos = held_seq[:, None] * BLK + inner[None, :]
    key_pos = held_pattern[:, :, None] * BLK + inner[None, None, :]
    allowed = live_slot[:, None, :, None] & (key_pos[:, None, :, :] <= query_pos[:, :, None, None])
    return (key_store, allowed)


def attend_tiles(query_held, grad_held, key_tiles, value_tiles, allowed):
    scaling = HEAD_SIZE ** (-0.5)
    scores = (
        jnp.einsum("biagd,bjkad->bagijk", query_held, key_tiles, preferred_element_type=jnp.float32)
        * scaling
    )
    scores = jnp.where(allowed[:, None, None], scores, -jnp.inf)
    row_max = jnp.max(scores, axis=(4, 5), keepdims=True)
    row_sum = jnp.sum(jnp.exp(scores - row_max), axis=(4, 5), keepdims=True)
    log_total = row_max + jnp.log(row_sum)
    prob_full = jnp.exp(scores - log_total)
    prob_low = prob_full.astype(jnp.bfloat16)
    attended_wide = jnp.einsum(
        "bagijk,bjkad->biagd", prob_low, value_tiles, preferred_element_type=jnp.float32
    )
    attended = attended_wide.astype(jnp.bfloat16)
    row_dot = jnp.sum(grad_held.astype(jnp.float32) * attended_wide, axis=-1)
    row_dot = jnp.transpose(row_dot, (0, 2, 3, 1))[..., None, None]
    grad_prob = jnp.einsum(
        "biagd,bjkad->bagijk", grad_held, value_tiles, preferred_element_type=jnp.float32
    )
    grad_score = (prob_full * (grad_prob - row_dot) * scaling).astype(jnp.bfloat16)
    query_grad = jnp.einsum(
        "bagijk,bjkad->biagd", grad_score, key_tiles, preferred_element_type=jnp.float32
    ).astype(jnp.bfloat16)
    key_grads = jnp.einsum(
        "bagijk,biagd->bjkad", grad_score, query_held, preferred_element_type=jnp.float32
    )
    value_grads = jnp.einsum(
        "bagijk,biagd->bjkad", prob_low, grad_held, preferred_element_type=jnp.float32
    )
    return (attended, query_grad, key_grads, value_grads)


def per_device(query_rows, key_rows, stored_value_rows, out_grad, block_table, pattern):
    ctx_index = lax.axis_index("ctx")
    per_dev = block_table.shape[1]
    blocks = pattern.shape[0]
    kv_local = key_rows.shape[1] // HEAD_SIZE
    groups = query_rows.shape[1] // key_rows.shape[1]
    held_rows = per_dev * BLK
    held_seq = lax.dynamic_index_in_dim(block_table, ctx_index, 0, keepdims=False)
    key_store, allowed = slot_layout(block_table, pattern, held_seq)
    key_all, value_all = (
        lax.all_gather(key_rows, "ctx", axis=0, tiled=True),
        lax.all_gather(stored_value_rows, "ctx", axis=0, tiled=True),
    )
    key_blocks = key_all.reshape(blocks, BLK, kv_local, HEAD_SIZE)
    value_blocks = value_all.reshape(blocks, BLK, kv_local, HEAD_SIZE)
    key_tiles = key_blocks[key_store]
    value_tiles = value_blocks[key_store]
    query_held = query_rows.reshape(per_dev, BLK, kv_local, groups, HEAD_SIZE)
    grad_held = out_grad.reshape(per_dev, BLK, kv_local, groups, HEAD_SIZE)
    attended, query_grad, key_grads, value_grads = attend_tiles(
        query_held, grad_held, key_tiles, value_tiles, allowed
    )
    flat_slots = key_store.reshape(-1)
    key_partial = (
        jnp.zeros((blocks, BLK, kv_local, HEAD_SIZE), jnp.float32)
        .at[flat_slots]
        .add(key_grads.reshape(-1, BLK, kv_local, HEAD_SIZE))
    )
    value_partial = (
        jnp.zeros((blocks, BLK, kv_local, HEAD_SIZE), jnp.float32)
        .at[flat_slots]
        .add(value_grads.reshape(-1, BLK, kv_local, HEAD_SIZE))
    )
    key_sum, value_sum = (
        lax.psum_scatter(
            key_partial.reshape(blocks * BLK, -1).astype(jnp.bfloat16),
            "ctx",
            scatter_dimension=0,
            tiled=True,
        ).astype(jnp.float32),
        lax.psum_scatter(
            value_partial.reshape(blocks * BLK, -1).astype(jnp.bfloat16),
            "ctx",
            scatter_dimension=0,
            tiled=True,
        ).astype(jnp.float32),
    )
    attended = attended.reshape(held_rows, -1)
    query_grad = query_grad.reshape(held_rows, -1)
    key_grad = key_sum.astype(jnp.bfloat16)
    value_grad = value_sum.astype(jnp.bfloat16)
    return (attended, query_grad, key_grad, value_grad)


def solution(mesh):
    in_specs = (
        P(("dp", "ctx"), "head"),
        P(("dp", "ctx"), "head"),
        P(("dp", "ctx"), "head"),
        P(("dp", "ctx"), "head"),
        P("dp", None),
        P("dp", None),
    )
    out_specs = (
        P(("dp", "ctx"), "head"),
        P(("dp", "ctx"), "head"),
        P(("dp", "ctx"), "head"),
        P(("dp", "ctx"), "head"),
    )
    return jax.shard_map(
        per_device, mesh=mesh, in_specs=in_specs, out_specs=out_specs, check_vma=False
    )
```

profile of v0, /device:TPU:2, one launch (start us, length us, event | category | flops | bytes accessed | tf_op | source)
XLA Modules:
  0.0 322.2 jit_solution(11498761475473287322)
XLA Ops:
  12.6 1.1 copy.98
  13.8 1.1 convert_bitcast_fusion
  14.9 1.1 copy.100
  17.1 1.4 copy.65
  19.0 54.9 %all-gather.5.cloned.1.call-done = bf16[4096,128]{1,0:T(8,128)(2,1)} async-done(((bf16[256,128]{1,0:T(8,128)(2,1)}), bf16[4096,128]{1,0:T(8,128)(2,1)}) %all-gather.5.cloned.1.call-update) | async-done | bytes 1048592 | tf_op jit(solution)/shard_map/all_gather | solution.py:79
  73.9 1.9 gather_fusion.1
  75.8 1.5 fusion.4
  77.4 2.3 exponential_reduce_fusion
  79.7 2.5 fusion.9
  82.2 1.5 broadcast.134.clone.1
  83.8 5.8 %scatter_fusion.1 = f32[32,128,128]{2,1,0:T(8,128)} fusion(f32[32,128,128]{2,1,0:T(8,128)} %broadcast.134.clone.1, s32[20]{0:T(128)S(1)} %fusion.17, f32[20,128,128]{2,1,0:T(8,128)S(1)} %bitcast.169), kind=kCustom, calls=%fused_computation.3 | custom fusion | flops 327680 | bytes 3932240 | tf_op jit(solution)/shard_map/scatter-add | solution.py:100
  89.6 3.0 convert_element_type.70
  92.9 41.2 %all-gather.3.cloned.1.call-done = bf16[4096,128]{1,0:T(8,128)(2,1)} async-done(((bf16[256,128]{1,0:T(8,128)(2,1)}), bf16[4096,128]{1,0:T(8,128)(2,1)}) %all-gather.3.cloned.1.call-update) | async-done | bytes 1048592 | tf_op jit(solution)/shard_map/all_gather | solution.py:80
  134.0 2.8 gather_fusion
  136.8 8.0 %multiply_reduce_fusion = (f32[2,128,8]{1,2,0:T(8,128)S(1)}, bf16[2,128,1,8,128]{1,4,3,0,2:T(8,128)(2,1)}) fusion(f32[2,128,1,8,128]{1,4,3,0,2:T(8,128)} %copy.65, bf16[2,10,128,128,1]{3,2,4,1,0:T(8,128)(2,1)} %bitcast.170, f32[2,10,128,128,8]{3,2,4,1,0:T(8,128)} %copy-done, f32[2,8,128]{2,1,0:T(8,128)S(1)} %log_add_fusion, ...), kind=kOutput, calls=%fused_computation.21 | convolution fusion | flops 682358784 | bytes 13058048 | tf_op jit(solution)/shard_map/bagijk,bjkad->biagd/dot_general | solution.py:47
  144.8 3.6 %fusion.6 = bf16[2,8,128,10,128]{2,4,1,3,0:T(8,128)(2,1)S(1)} fusion(f32[2,10,128,128,8]{3,2,4,1,0:T(8,128)S(1)} %bitcast.157, f32[2,8,128]{2,1,0:T(8,128)S(1)} %bitcast.175, f32[2,8,128]{2,1,0:T(8,128)S(1)} %log_add_fusion, pred[2,128,10,128]{1,3,2,0:T(8,128)(4,1)S(1)} %copy-done.3, bf16[2,10,128,128,1]{3,2,4,1,0:T(8,128)(2,1)S(1)} %bitcast.171, ...), kind=kOutput, calls=%fused_computation.14 | convolution fusion | flops 689438720 | bytes 17252352 | tf_op jit(solution)/shard_map/biagd,bjkad->bagijk/dot_general | solution.py:53
  148.5 2.3 copy-done.1
  150.8 2.6 fusion.12
  153.6 4.4 %scatter_fusion = f32[32,128,128]{2,1,0:T(8,128)S(1)} fusion(f32[32,128,128]{2,1,0:T(8,128)S(1)} %broadcast.134.clone, s32[20]{0:T(128)S(1)} %fusion.17, f32[20,128,128]{2,1,0:T(8,128)} %bitcast.160), kind=kCustom, calls=%fused_computation.2 | custom fusion | flops 327680 | bytes 3932240 | tf_op jit(solution)/shard_map/scatter-add | solution.py:95
  158.1 1.2 convert_element_type.69
  159.3 3.5 %fusion.8 = bf16[2,128,1,8,128]{1,4,3,0,2:T(8,128)(2,1)S(1)} fusion(bf16[2,10,128,128,1]{3,2,4,1,0:T(8,128)(2,1)S(1)} %bitcast.159, bf16[2,8,128,10,128]{2,4,1,3,0:T(8,128)(2,1)} %copy-done.1), kind=kOutput, calls=%fused_computation.19 | convolution fusion | flops 671350784 | bytes 6422528 | tf_op jit(solution)/shard_map/bagijk,bjkad->biagd/dot_general | solution.py:57
  163.4 1.2 copy_bitcast_fusion
  164.6 60.9 %reduce-scatter.5.cloned.1.call-done = bf16[256,128]{1,0:T(8,128)(2,1)} async-done(((bf16[4096,128]{1,0:T(8,128)(2,1)}), bf16[256,128]{1,0:T(8,128)(2,1)}) %reduce-scatter.5.cloned.1.call-update) | async-done | bytes 65552 | tf_op jit(solution)/shard_map/reduce_scatter | solution.py:109
  225.5 90.2 %reduce-scatter.3.cloned.1.call-done = bf16[256,128]{1,0:T(8,128)(2,1)} async-done(((bf16[4096,128]{1,0:T(8,128)(2,1)}), bf16[256,128]{1,0:T(8,128)(2,1)}) %reduce-scatter.3.cloned.1.call-update) | async-done | bytes 65552 | tf_op jit(solution)/shard_map/reduce_scatter | solution.py:103
  (59 shorter events, 8.1 us)
Async XLA Ops:
  7.2 66.7 %all-gather.5.cloned.1.call-start = ((), (), s32[]{:S(2)}) async-start(), calls=%async_computation.3 | async-start | bytes 1114112 | tf_op jit(solution)/shard_map/all_gather | solution.py:79
  7.9 126.1 %all-gather.3.cloned.1.call-start = ((), (), s32[]{:S(2)}) async-start(), calls=%async_computation.2 | async-start | bytes 1114112 | tf_op jit(solution)/shard_map/all_gather | solution.py:80
  8.6 216.8 %reduce-scatter.5.cloned.1.call-start = ((), (), s32[]{:S(2)}) async-start(), calls=%async_computation.5 | async-start | bytes 1114112 | tf_op jit(solution)/shard_map/reduce_scatter | solution.py:109
  19.0 64.8 %copy-start.2 = (pred[2,128,10,128]{1,3,2,0:T(8,128)(4,1)}, pred[2,128,10,128]{1,3,2,0:T(8,128)(4,1)S(1)}, u32[]{:S(2)}) copy-start(pred[2,128,10,128]{1,3,2,0:T(8,128)(4,1)S(1)} %compare_and_fusion) | copy-start | bytes 983044
  75.8 3.9 %copy-start.5 = (bf16[2,128,8,128,1]{3,2,1,0,4:T(8,128)(2,1)S(1)}, bf16[2,128,8,128,1]{3,2,1,0,4:T(8,128)(2,1)}, u32[]{:S(2)}) copy-start(bf16[2,128,8,128,1]{3,2,1,0,4:T(8,128)(2,1)} %bitcast_bitcast_fusion) | copy-start | bytes 1572868
  77.4 4.9 %copy-start = (f32[2,10,128,128,8]{3,2,4,1,0:T(8,128)}, f32[2,10,128,128,8]{3,2,4,1,0:T(8,128)S(1)}, u32[]{:S(2)}) copy-start(f32[2,10,128,128,8]{3,2,4,1,0:T(8,128)S(1)} %get-tuple-element.7) | copy-start | bytes 31457284
  89.6 55.1 %slice-start = ((s8[10485760]{0:T(1024)(128)(4,1)}), s8[2097152]{0:T(1024)(128)(4,1)S(1)}, s32[]{:S(2)}) async-start(s8[10485760]{0:T(1024)(128)(4,1)} %bitcast.156), calls=%async_computation.6 | async-start | bytes 4194304
  92.6 223.0 %reduce-scatter.3.cloned.1.call-start = ((), (), s32[]{:S(2)}) async-start(), calls=%async_computation.4 | async-start | bytes 1114112 | tf_op jit(solution)/shard_map/reduce_scatter | solution.py:103
  136.8 8.0 %copy-start.3 = (pred[2,128,10,128]{1,3,2,0:T(8,128)(4,1)S(1)}, pred[2,128,10,128]{1,3,2,0:T(8,128)(4,1)}, u32[]{:S(2)}) copy-start(pred[2,128,10,128]{1,3,2,0:T(8,128)(4,1)} %copy-done.2) | copy-start | bytes 983044
  136.8 8.0 %copy-start.4 = (bf16[20,128,128]{2,1,0:T(8,128)(2,1)S(1)}, bf16[20,128,128]{2,1,0:T(8,128)(2,1)}, u32[]{:S(2)}) copy-start(bf16[20,128,128]{2,1,0:T(8,128)(2,1)} %gather_fusion) | copy-start | bytes 1966084
  136.8 8.0 %copy-start.6 = (bf16[2,128,8,128,1]{3,2,1,0,4:T(8,128)(2,1)S(1)}, bf16[2,128,8,128,1]{3,2,1,0,4:T(8,128)(2,1)}, u32[]{:S(2)}) copy-start(bf16[2,128,8,128,1]{3,2,1,0,4:T(8,128)(2,1)} %bitcast_bitcast_fusion) | copy-start | bytes 1572868
  136.8 8.0 %slice-start.1 = ((s8[10485760]{0:T(1024)(128)(4,1)}), s8[4194304]{0:T(1024)(128)(4,1)S(1)}, s32[]{:S(2)}) async-start(s8[10485760]{0:T(1024)(128)(4,1)} %bitcast.156), calls=%async_computation.7 | async-start | bytes 8388608
  136.8 8.0 %slice-start.2 = ((s8[10485760]{0:T(1024)(128)(4,1)}), s8[4194304]{0:T(1024)(128)(4,1)S(1)}, s32[]{:S(2)}) async-start(s8[10485760]{0:T(1024)(128)(4,1)} %bitcast.156), calls=%async_computation.8 | async-start | bytes 8388608
  148.5 2.3 copy-start.1
  153.4 9.7 %copy-start.7 = (bf16[2,128,1,8,128]{1,4,3,0,2:T(8,128)(2,1)S(1)}, bf16[2,128,1,8,128]{1,4,3,0,2:T(8,128)(2,1)}, u32[]{:S(2)}) copy-start(bf16[2,128,1,8,128]{1,4,3,0,2:T(8,128)(2,1)} %get-tuple-element.5) | copy-start | bytes 1572868
Sparse Core Ops, SparseCore 0:
  11.3 62.5 all-gather.4
  77.2 56.8 all-gather.2
  139.3 86.1 reduce-scatter.4
  231.3 84.2 reduce-scatter.2
where the time goes:
time: 323 us; the launch traced here: 322 us
  waiting for transfers between devices  249 us (77%)
  matrix products  21.8 us (7%)
  other arithmetic  20.2 us (6%)
  local copies, waits for them, and re-layouts  17.3 us (5%)
  between operations  14 us (4%)
    reduce_scatter x1, waiting for transfers between devices, per_device(): lax.psum_scatter(key_partial.reshape(blocks * BLK, -1).astype(jnp.bfloat1...  90.2 us
    reduce_scatter x1, waiting for transfers between devices, per_device(): lax.psum_scatter(value_partial.reshape(blocks * BLK, -1).astype(jnp.bfloa...  60.9 us
    all_gather x1, waiting for transfers between devices, per_device(): lax.all_gather(key_rows, 'ctx', axis=0, tiled=True)  54.9 us
    all_gather x1, waiting for transfers between devices, per_device(): lax.all_gather(stored_value_rows, 'ctx', axis=0, tiled=True)  41.2 us
    dot_general x1, matrix products, attend_tiles(): jnp.einsum('bagijk,bjkad->biagd', prob_low, value_tiles, preferred_elemen...  7.98 us
  transfers between devices with their start and end apart: 4, of which 4 were waited for; matrix products, arithmetic and copies ran while one was open for 18% of the time, Pallas kernels for 0%

commit v1 on v0

--- a/solution.py
+++ b/solution.py
@@ -2,6 +2,7 @@
 import jax.numpy as jnp
 from jax import lax
 from jax.sharding import PartitionSpec as P
+from jax.lax import all_to_all, axis_size
 
 HEAD_SIZE = 128
 BLK = 128
@@ -76,7 +77,15 @@
     held_seq = lax.dynamic_index_in_dim(block_table, ctx_index, 0, keepdims=False)
     key_store, allowed = slot_layout(block_table, pattern, held_seq)
     key_all, value_all = (
-        lax.all_gather(key_rows, "ctx", axis=0, tiled=True),
+        jnp.concatenate(
+            all_to_all(
+                jnp.stack([key_rows for _ in range(axis_size("ctx"))]),
+                axis_name="ctx",
+                split_axis=0,
+                concat_axis=0,
+            ),
+            axis=0,
+        ),
         lax.all_gather(stored_value_rows, "ctx", axis=0, tiled=True),
     )
     key_blocks = key_all.reshape(blocks, BLK, kv_local, HEAD_SIZE)

time: 323 us -> 278 us (0.86)
  waiting for transfers between devices: 249 us -> 191 us
  starting transfers between devices: 0.34 us -> 10.4 us
    all_gather x1 -> x0, waiting for transfers between devices: 54.9 us -> none  [per_device(): lax.all_gather(key_rows, 'ctx', axis=0, tiled=True)]
    all_gather x1, waiting for transfers between devices: 41.2 us -> 24.6 us  [per_device(): lax.all_gather(stored_value_rows, 'ctx', axis=0, tiled=True)]
    all_to_all x0 -> x1, waiting for transfers between devices: none -> 14.5 us  [per_device(): all_to_all(jnp.stack([key_rows for _ in range(axis_size('ctx'))]), axis_n...]
    all_to_all x0 -> x1, starting transfers between devices: none -> 10.1 us  [per_device(): all_to_all(jnp.stack([key_rows for _ in range(axis_size('ctx'))]), axis_n...]
  transfers between devices with their start and end apart: 4 -> 4, of which waited for: 4 -> 4; matrix products, arithmetic and copies ran while one was open for 18% -> 21% of each run, Pallas kernels for 0% -> 0%
where the time goes in v1:
time: 278 us; the launch traced here: 277 us
  waiting for transfers between devices  191 us (69%)
  matrix products  21.8 us (8%)
  other arithmetic  20.2 us (7%)
  local copies, waits for them, and re-layouts  20 us (7%)
  between operations  14 us (5%)
  starting transfers between devices  10.4 us (4%)
    reduce_scatter x1, waiting for transfers between devices, per_device(): lax.psum_scatter(key_partial.reshape(blocks * BLK, -1).astype(jnp.bfloat1...  90.3 us
    reduce_scatter x1, waiting for transfers between devices, per_device(): lax.psum_scatter(value_partial.reshape(blocks * BLK, -1).astype(jnp.bfloa...  60.9 us
    all_gather x1, waiting for transfers between devices, per_device(): lax.all_gather(stored_value_rows, 'ctx', axis=0, tiled=True)  24.6 us
    all_to_all x1, waiting for transfers between devices, per_device(): all_to_all(jnp.stack([key_rows for _ in range(axis_size('ctx'))]), axis_n...  14.5 us
    all_to_all x1, starting transfers between devices, per_device(): all_to_all(jnp.stack([key_rows for _ in range(axis_size('ctx'))]), axis_n...  10.1 us
    dot_general x1, matrix products, attend_tiles(): jnp.einsum('bagijk,bjkad->biagd', prob_low, value_tiles, preferred_elemen...  7.98 us
    unnamed x26, local copies, waits for them, and re-layouts  6.38 us
    scatter-add x1, other arithmetic, per_device(): value_partial = jnp.zeros((blocks, BLK, kv_local, HEAD_SIZE), jnp.float32...  5.85 us
  transfers between devices with their start and end apart: 4, of which 4 were waited for; matrix products, arithmetic and copies ran while one was open for 21% of the time, Pallas kernels for 0%

profile of v1, /device:TPU:2, one launch (start us, length us, event | category | flops | bytes accessed | tf_op | source)
XLA Modules:
  0.0 277.5 jit_solution(11878013334943655799)
XLA Ops:
  7.2 2.0 stack.2
  9.2 10.1 %all-to-all-start = ((bf16[16,256,128]{2,1,0:T(8,128)(2,1)}), bf16[16,256,128]{2,1,0:T(8,128)(2,1)S(1)}, u32[]{:S(2)}, u32[]{:S(2)}) async-start(bf16[16,256,128]{2,1,0:T(8,128)(2,1)} %stack.2), calls=%async_computation | async-start | bytes 2097152 | tf_op jit(solution)/shard_map/all_to_all | solution.py:81
  26.1 1.9 copy.97
  28.2 1.4 copy.60
  30.4 2.0 bitcast_bitcast_fusion
  32.3 14.5 %all-to-all-done = bf16[16,256,128]{2,1,0:T(8,128)(2,1)S(1)} async-done(((bf16[16,256,128]{2,1,0:T(8,128)(2,1)}), bf16[16,256,128]{2,1,0:T(8,128)(2,1)S(1)}, u32[]{:S(2)}, u32[]{:S(2)}) %all-to-all-start) | async-done | bytes 1048608 | tf_op jit(solution)/shard_map/all_to_all | solution.py:81
  47.5 1.5 fusion.4
  49.1 2.3 exponential_reduce_fusion
  51.4 2.5 fusion.9
  53.9 1.5 broadcast.136.clone.1
  55.5 5.8 %scatter_fusion.1 = f32[32,128,128]{2,1,0:T(8,128)} fusion(f32[32,128,128]{2,1,0:T(8,128)} %broadcast.136.clone.1, s32[20]{0:T(128)S(1)} %fusion.17, f32[20,128,128]{2,1,0:T(8,128)S(1)} %bitcast.167), kind=kCustom, calls=%fused_computation.3 | custom fusion | flops 327680 | bytes 3932240 | tf_op jit(solution)/shard_map/scatter-add | solution.py:109
  61.3 3.0 %convert_element_type.70 = bf16[32,128,128]{2,1,0:T(8,128)(2,1)} convert(f32[32,128,128]{2,1,0:T(8,128)} %scatter_fusion.1) | non-fusion elementwise | flops 524288 | bytes 3145728 | tf_op jit(solution)/shard_map/convert_element_type | solution.py:119
  64.6 24.6 %all-gather.2.cloned.1.call-done = bf16[4096,128]{1,0:T(8,128)(2,1)} async-done(((bf16[256,128]{1,0:T(8,128)(2,1)}), bf16[4096,128]{1,0:T(8,128)(2,1)}) %all-gather.2.cloned.1.call-update) | async-done | bytes 1048592 | tf_op jit(solution)/shard_map/all_gather | solution.py:89
  89.2 2.8 gather_fusion
  91.9 8.0 %multiply_reduce_fusion = (f32[2,128,8]{1,2,0:T(8,128)S(1)}, bf16[2,128,1,8,128]{1,4,3,0,2:T(8,128)(2,1)}) fusion(f32[2,128,1,8,128]{1,4,3,0,2:T(8,128)} %copy.60, bf16[2,10,128,128,1]{3,2,4,1,0:T(8,128)(2,1)} %bitcast.168, f32[2,10,128,128,8]{3,2,4,1,0:T(8,128)} %copy-done, f32[2,8,128]{2,1,0:T(8,128)S(1)} %log_add_fusion, ...), kind=kOutput, calls=%fused_computation.21 | convolution fusion | flops 682358784 | bytes 13058048 | tf_op jit(solution)/shard_map/bagijk,bjkad->biagd/dot_general | solution.py:48
  100.0 3.6 %fusion.6 = bf16[2,8,128,10,128]{2,4,1,3,0:T(8,128)(2,1)S(1)} fusion(f32[2,10,128,128,8]{3,2,4,1,0:T(8,128)S(1)} %bitcast.154, f32[2,8,128]{2,1,0:T(8,128)S(1)} %bitcast.172, f32[2,8,128]{2,1,0:T(8,128)S(1)} %log_add_fusion, pred[2,128,10,128]{1,3,2,0:T(8,128)(4,1)S(1)} %copy-done.3, bf16[2,10,128,128,1]{3,2,4,1,0:T(8,128)(2,1)S(1)} %bitcast.169, ...), kind=kOutput, calls=%fused_computation.14 | convolution fusion | flops 689438720 | bytes 17252352 | tf_op jit(solution)/shard_map/biagd,bjkad->bagijk/dot_general | solution.py:54
  103.6 2.3 copy-done.1
  105.9 2.6 fusion.12
  108.8 4.4 %scatter_fusion = f32[32,128,128]{2,1,0:T(8,128)S(1)} fusion(f32[32,128,128]{2,1,0:T(8,128)S(1)} %broadcast.136.clone, s32[20]{0:T(128)S(1)} %fusion.17, f32[20,128,128]{2,1,0:T(8,128)} %bitcast.157), kind=kCustom, calls=%fused_computation.2 | custom fusion | flops 327680 | bytes 3932240 | tf_op jit(solution)/shard_map/scatter-add | solution.py:104
  113.2 1.2 convert_element_type.69
  114.4 3.5 %fusion.8 = bf16[2,128,1,8,128]{1,4,3,0,2:T(8,128)(2,1)S(1)} fusion(bf16[2,10,128,128,1]{3,2,4,1,0:T(8,128)(2,1)S(1)} %bitcast.156, bf16[2,8,128,10,128]{2,4,1,3,0:T(8,128)(2,1)} %copy-done.1), kind=kOutput, calls=%fused_computation.19 | convolution fusion | flops 671350784 | bytes 6422528 | tf_op jit(solution)/shard_map/bagijk,bjkad->biagd/dot_general | solution.py:58
  118.5 1.2 copy_bitcast_fusion
  119.7 60.9 %reduce-scatter.5.cloned.1.call-done = bf16[256,128]{1,0:T(8,128)(2,1)} async-done(((bf16[4096,128]{1,0:T(8,128)(2,1)}), bf16[256,128]{1,0:T(8,128)(2,1)}) %reduce-scatter.5.cloned.1.call-update) | async-done | bytes 65552 | tf_op jit(solution)/shard_map/reduce_scatter | solution.py:118
  180.6 90.3 %reduce-scatter.3.cloned.1.call-done = bf16[256,128]{1,0:T(8,128)(2,1)} async-done(((bf16[4096,128]{1,0:T(8,128)(2,1)}), bf16[256,128]{1,0:T(8,128)(2,1)}) %reduce-scatter.3.cloned.1.call-update) | async-done | bytes 65552 | tf_op jit(solution)/shard_map/reduce_scatter | solution.py:112
  (59 shorter events, 9.5 us)
Async XLA Ops:
  9.2 37.6 %all-to-all-start = ((bf16[16,256,128]{2,1,0:T(8,128)(2,1)}), bf16[16,256,128]{2,1,0:T(8,128)(2,1)S(1)}, u32[]{:S(2)}, u32[]{:S(2)}) async-start(bf16[16,256,128]{2,1,0:T(8,128)(2,1)} %stack.2), calls=%async_computation | async-start | bytes 2097152 | tf_op jit(solution)/shard_map/all_to_all | solution.py:81
  19.3 69.9 %all-gather.2.cloned.1.call-start = ((), (), s32[]{:S(2)}) async-start(), calls=%async_computation.3 | async-start | bytes 1114112 | tf_op jit(solution)/shard_map/all_gather | solution.py:89
  20.0 160.6 %reduce-scatter.5.cloned.1.call-start = ((), (), s32[]{:S(2)}) async-start(), calls=%async_computation.5 | async-start | bytes 1114112 | tf_op jit(solution)/shard_map/reduce_scatter | solution.py:118
  30.3 25.2 %copy-start.2 = (pred[2,128,10,128]{1,3,2,0:T(8,128)(4,1)}, pred[2,128,10,128]{1,3,2,0:T(8,128)(4,1)S(1)}, u32[]{:S(2)}) copy-start(pred[2,128,10,128]{1,3,2,0:T(8,128)(4,1)S(1)} %compare_and_fusion) | copy-start | bytes 983044
  47.5 3.9 %copy-start.5 = (bf16[2,128,8,128,1]{3,2,1,0,4:T(8,128)(2,1)S(1)}, bf16[2,128,8,128,1]{3,2,1,0,4:T(8,128)(2,1)}, u32[]{:S(2)}) copy-start(bf16[2,128,8,128,1]{3,2,1,0,4:T(8,128)(2,1)} %bitcast_bitcast_fusion) | copy-start | bytes 1572868
  49.1 4.9 %copy-start = (f32[2,10,128,128,8]{3,2,4,1,0:T(8,128)}, f32[2,10,128,128,8]{3,2,4,1,0:T(8,128)S(1)}, u32[]{:S(2)}) copy-start(f32[2,10,128,128,8]{3,2,4,1,0:T(8,128)S(1)} %get-tuple-element.7) | copy-start | bytes 31457284
  61.3 38.6 %slice-start = ((s8[10485760]{0:T(1024)(128)(4,1)}), s8[2097152]{0:T(1024)(128)(4,1)S(1)}, s32[]{:S(2)}) async-start(s8[10485760]{0:T(1024)(128)(4,1)} %bitcast.153), calls=%async_computation.6 | async-start | bytes 4194304
  64.3 206.6 %reduce-scatter.3.cloned.1.call-start = ((), (), s32[]{:S(2)}) async-start(), calls=%async_computation.4 | async-start | bytes 1114112 | tf_op jit(solution)/shard_map/reduce_scatter | solution.py:112
  91.9 8.0 %copy-start.3 = (pred[2,128,10,128]{1,3,2,0:T(8,128)(4,1)S(1)}, pred[2,128,10,128]{1,3,2,0:T(8,128)(4,1)}, u32[]{:S(2)}) copy-start(pred[2,128,10,128]{1,3,2,0:T(8,128)(4,1)} %copy-done.2) | copy-start | bytes 983044
  91.9 8.0 %copy-start.4 = (bf16[20,128,128]{2,1,0:T(8,128)(2,1)S(1)}, bf16[20,128,128]{2,1,0:T(8,128)(2,1)}, u32[]{:S(2)}) copy-start(bf16[20,128,128]{2,1,0:T(8,128)(2,1)} %gather_fusion) | copy-start | bytes 1966084
  91.9 8.0 %copy-start.6 = (bf16[2,128,8,128,1]{3,2,1,0,4:T(8,128)(2,1)S(1)}, bf16[2,128,8,128,1]{3,2,1,0,4:T(8,128)(2,1)}, u32[]{:S(2)}) copy-start(bf16[2,128,8,128,1]{3,2,1,0,4:T(8,128)(2,1)} %bitcast_bitcast_fusion) | copy-start | bytes 1572868
  91.9 8.0 %slice-start.1 = ((s8[10485760]{0:T(1024)(128)(4,1)}), s8[4194304]{0:T(1024)(128)(4,1)S(1)}, s32[]{:S(2)}) async-start(s8[10485760]{0:T(1024)(128)(4,1)} %bitcast.153), calls=%async_computation.7 | async-start | bytes 8388608
  91.9 8.0 %slice-start.2 = ((s8[10485760]{0:T(1024)(128)(4,1)}), s8[4194304]{0:T(1024)(128)(4,1)S(1)}, s32[]{:S(2)}) async-start(s8[10485760]{0:T(1024)(128)(4,1)} %bitcast.153), calls=%async_computation.8 | async-start | bytes 8388608
  103.6 2.3 copy-start.1
  108.5 9.7 %copy-start.7 = (bf16[2,128,1,8,128]{1,4,3,0,2:T(8,128)(2,1)S(1)}, bf16[2,128,1,8,128]{1,4,3,0,2:T(8,128)(2,1)}, u32[]{:S(2)}) copy-start(bf16[2,128,1,8,128]{1,4,3,0,2:T(8,128)(2,1)} %get-tuple-element.5) | copy-start | bytes 1572868
Sparse Core Ops, SparseCore 0:
  23.4 65.7 all-gather.1
  94.4 86.1 reduce-scatter.4
  186.6 84.2 reduce-scatter.2
